TPU v7x, 32 devices: a whole 2x2x4 slice. The times are simulated.
32 devices in a mesh: brick: 8 (over z, y), vec: 4 (over x, core).
Axes of the slice: x: 2, y: 2, z: 4, core: 2. Of those that a mesh axis runs over, the one named last changes fastest.
Arguments:
- right_side: float32 [4, 4, 32, 128, 128], P('vec', None, 'brick'), may hold values from -6 to 6
- diffusivity: float32 [32, 128, 128], P('brick'), may hold values from 0.3 to 3
Outputs:
- precond: float32 [4, 4, 32, 128, 128], P('vec', None, 'brick')
- gram: float32 [4, 4], P('vec')
All inputs are finite; a program needn't handle non-finite values.
Results may differ from a plain program's by a relative error of at most 0.0003.
Values may be sent and summed in bfloat16 or wider, within the bound.
A program may use at most 64 MiB of HBM per device.

v0:
```python
import jax
import jax.numpy as jnp
from jax import lax
from jax.sharding import PartitionSpec as P

SWEEPS = 6


shift_value = 0.1
damping = 0.8


def extended(block, sides, width):
    for axis, dim in sides:
        count = lax.axis_size(axis)
        forward = [(i, i + 1) for i in range(count - 1)]
        backward = [(target, source) for source, target in forward]
        low = lax.ppermute(
            lax.slice_in_dim(block, block.shape[dim] - width, None, axis=dim), axis, forward
        )
        high = lax.ppermute(lax.slice_in_dim(block, 0, width, axis=dim), axis, backward)
        block = jnp.concatenate([low, block, high], axis=dim)
    return block


def passed_along(value, axis, steps):
    count = lax.axis_size(axis)
    pairs = [(source, (source + steps) % count) for source in range(count)]
    return lax.ppermute(value, axis, pairs)


def neighbours(padded):
    middle = padded[..., 1:-1, :, :]
    total = padded[..., 2:, :, :] + padded[..., :-2, :, :]
    lead = [(0, 0)] * (middle.ndim - 2)
    side_y = jnp.pad(middle, lead + [(1, 1), (0, 0)])
    total = total + side_y[..., 2:, :] + side_y[..., :-2, :]
    side_z = jnp.pad(middle, lead + [(0, 0), (1, 1)])
    total = total + side_z[..., 2:] + side_z[..., :-2]
    return total


def operate(padded, kappa, scale):
    middle = padded[..., 1:-1, :, :]
    return shift_value * middle + scale * kappa * (6.0 * middle - neighbours(padded))


def pair_table(cols):
    fine = jnp.arange(cols, dtype=jnp.int32)
    coarse = jnp.arange(cols // 2, dtype=jnp.int32)
    return jnp.where(fine[:, None] // 2 == coarse[None, :], 1.0, 0.0).astype(jnp.float32)


def restrict(field):
    cols = field.shape[-1]
    summed = field[..., 0::2, :, :] + field[..., 1::2, :, :]
    summed = summed[..., 0::2, :] + summed[..., 1::2, :]
    halved = jnp.dot(
        summed,
        pair_table(cols),
        precision=lax.Precision.HIGHEST,
        preferred_element_type=jnp.float32,
    )
    return halved * 0.125


def prolong(field):
    lead = field.shape[:-3]
    planes, rows, cols = field.shape[-3:]
    table = pair_table(2 * cols).T
    wide_cols = jnp.dot(
        field, table, precision=lax.Precision.HIGHEST, preferred_element_type=jnp.float32
    )
    wide = jnp.broadcast_to(
        wide_cols[..., :, None, :, None, :], lead + (planes, 2, rows, 2, 2 * cols)
    )
    return wide.reshape(lead + (planes * 2, rows * 2, cols * 2))


def slab_halo(field):
    return extended(field, (("brick", 2),), 1)


def local(right_side, diffusivity):
    kappa1 = restrict(diffusivity)
    kappa2 = restrict(kappa1)
    diag0 = shift_value + 6.0 * diffusivity
    diag1 = shift_value + 6.0 * 0.25 * kappa1
    diag2 = shift_value + 6.0 * 0.0625 * kappa2
    level0 = damping * right_side / diag0
    resid0 = right_side - operate(slab_halo(level0), diffusivity, 1.0)
    right1 = restrict(resid0)
    level1 = damping * right1 / diag1
    resid1 = right1 - operate(slab_halo(level1), kappa1, 0.25)
    right2 = restrict(resid1)
    level2 = damping * right2 / diag2
    for sweep in range(SWEEPS - 1):
        padded = extended(level2, (("brick", 2),), 1)
        level2 = level2 + damping * (right2 - operate(padded, kappa2, 0.0625)) / diag2
    level1 = level1 + prolong(level2)
    level1 = level1 + damping * (right1 - operate(slab_halo(level1), kappa1, 0.25)) / diag1
    level0 = level0 + prolong(level1)
    precond = level0 + damping * (right_side - operate(slab_halo(level0), diffusivity, 1.0)) / diag0
    rounded = precond.astype(jnp.bfloat16)
    own_count = rounded.shape[0]
    group_size = lax.axis_size("vec")
    all_count = own_count * group_size
    own_index = lax.axis_index("vec")
    row_start = own_index * own_count
    own_block = jnp.einsum("afxyz,bfxyz->ab", rounded, rounded, preferred_element_type=jnp.float32)
    contributions = jnp.zeros((all_count, all_count), jnp.float32)
    contributions = lax.dynamic_update_slice(contributions, own_block, (row_start, row_start))
    current = rounded
    for distance in range(1, group_size // 2 + 1):
        current = passed_along(current, "vec", -1)
        pair_block = jnp.einsum(
            "afxyz,bfxyz->ab", rounded, current, preferred_element_type=jnp.float32
        )
        if 2 * distance == group_size:
            keeper = jnp.where(own_index < group_size // 2, 1.0, 0.0).astype(jnp.float32)
            pair_block = pair_block * keeper
        col_start = (own_index + distance) % group_size * own_count
        contributions = lax.dynamic_update_slice(contributions, pair_block, (row_start, col_start))
        contributions = lax.dynamic_update_slice(
            contributions, pair_block.T, (col_start, row_start)
        )
    total = lax.psum(contributions, ("brick", "vec"))
    gram = lax.dynamic_slice_in_dim(total, row_start, own_count, 0)
    return (precond, gram)


def solution(mesh):
    placed = (P("vec", None, "brick", None, None), P("brick", None, None))
    return jax.shard_map(
        local,
        mesh=mesh,
        in_specs=placed,
        out_specs=(P("vec", None, "brick", None, None), P("vec", None)),
        check_vma=False,
    )
```

profile of v0, /device:TPU:0, one launch (start us, length us, event | category | flops | bytes accessed | tf_op | source)
XLA Modules:
  0.0 174.1 jit_solution(16888773252168882581)
XLA Ops:
  1.6 1.4 multiply_divide_fusion
  3.1 1.4 collective-permute-start
  4.5 6.2 %collective-permute-start.1 = (f32[1,4,1,128,128]{4,3,2,1,0:T(8,128)S(1)}, f32[1,4,1,128,128]{4,3,2,1,0:T(8,128)}, u32[]{:S(2)}, u32[]{:S(2)}) collective-permute-start(f32[1,4,1,128,128]{4,3,2,1,0:T(8,128)S(1)} %get-tuple-element.10), channel_id=1, source_target_pairs={{0,4},{4,8},{8,12},{12,16},{16,20},{20,24},{24,28},{1,5},{5,9},{9,... | collective-permute-start | bytes 786440 | tf_op jit(solution)/shard_map/ppermute | solution.py:18
  11.1 3.4 %collective-permute-done = f32[1,4,1,128,128]{4,3,2,1,0:T(8,128)} collective-permute-done((f32[1,4,1,128,128]{4,3,2,1,0:T(8,128)S(1)}, f32[1,4,1,128,128]{4,3,2,1,0:T(8,128)}, u32[]{:S(2)}, u32[]{:S(2)}) %collective-permute-start) | collective-permute-done | bytes 262176 | tf_op jit(solution)/shard_map/ppermute | solution.py:21
  14.5 5.7 %collective-permute-done.1 = f32[1,4,1,128,128]{4,3,2,1,0:T(8,128)} collective-permute-done((f32[1,4,1,128,128]{4,3,2,1,0:T(8,128)S(1)}, f32[1,4,1,128,128]{4,3,2,1,0:T(8,128)}, u32[]{:S(2)}, u32[]{:S(2)}) %collective-permute-start.1) | collective-permute-done | bytes 262176 | tf_op jit(solution)/shard_map/ppermute | solution.py:18
  20.2 1.8 %fusion.7 = f32[1,4,4,128,128]{4,3,2,1,0:T(8,128)S(1)} fusion(f32[1,4,4,128,128]{4,3,2,1,0:T(8,128)S(1)} %copy-done, f32[1,4,4,128,128]{4,3,2,1,0:T(8,128)S(1)} %multiply_divide_fusion, f32[1,4,1,128,128]{4,3,2,1,0:T(8,128)} %collective-permute-done.1, f32[1,4,1,128,128]{4,3,2,1,0:T(8,128)} %collective-permute-done, f32[4,128,128]{2,1,0:T(8,128)S(1)} %copy-done.1), kind=kLoop, calls=%fused_computation.18 | loop fusion | flops 3407872 | bytes 3932160 | tf_op jit(solution)/shard_map/sub | solution.py:91
  22.8 1.3 collective-permute-start.2
  24.1 5.1 %collective-permute-start.3 = (f32[1,4,1,64,64]{4,3,2,1,0:T(8,128)S(1)}, f32[1,4,1,64,64]{4,3,2,1,0:T(8,128)S(1)}, u32[]{:S(2)}, u32[]{:S(2)}) collective-permute-start(f32[1,4,1,64,64]{4,3,2,1,0:T(8,128)S(1)} %get-tuple-element.14), channel_id=1, source_target_pairs={{0,4},{4,8},{8,12},{12,16},{16,20},{20,24},{24,28},{1,5},{5,9},{9,... | collective-permute-start | bytes 196616 | tf_op jit(solution)/shard_map/ppermute | solution.py:18
  29.4 1.6 collective-permute-done.2
  31.0 3.0 %collective-permute-done.3 = f32[1,4,1,64,64]{4,3,2,1,0:T(8,128)S(1)} collective-permute-done((f32[1,4,1,64,64]{4,3,2,1,0:T(8,128)S(1)}, f32[1,4,1,64,64]{4,3,2,1,0:T(8,128)S(1)}, u32[]{:S(2)}, u32[]{:S(2)}) %collective-permute-start.3) | collective-permute-done | bytes 65568 | tf_op jit(solution)/shard_map/ppermute | solution.py:18
  34.7 1.3 collective-permute-start.4
  36.0 5.0 %collective-permute-start.5 = (f32[1,4,1,32,32]{4,3,1,2,0:T(8,128)S(1)}, f32[1,4,1,32,32]{4,3,1,2,0:T(8,128)S(1)}, u32[]{:S(2)}, u32[]{:S(2)}) collective-permute-start(f32[1,4,1,32,32]{4,3,1,2,0:T(8,128)S(1)} %fusion.130), channel_id=1, source_target_pairs={{0,4},{4,8},{8,12},{12,16},{16,20},{20,24},{24,28},{1,5},{5,9},{9,... | collective-permute-start | bytes 49160 | tf_op jit(solution)/shard_map/ppermute | solution.py:18
  41.3 1.8 %collective-permute-done.5 = f32[1,4,1,32,32]{4,3,1,2,0:T(8,128)S(1)} collective-permute-done((f32[1,4,1,32,32]{4,3,1,2,0:T(8,128)S(1)}, f32[1,4,1,32,32]{4,3,1,2,0:T(8,128)S(1)}, u32[]{:S(2)}, u32[]{:S(2)}) %collective-permute-start.5) | collective-permute-done | bytes 16416 | tf_op jit(solution)/shard_map/ppermute | solution.py:18
  44.5 5.2 %collective-permute-start.7 = (f32[1,4,1,32,32]{4,3,1,2,0:T(8,128)S(1)}, f32[1,4,1,32,32]{4,3,1,2,0:T(8,128)S(1)}, u32[]{:S(2)}, u32[]{:S(2)}) collective-permute-start(f32[1,4,1,32,32]{4,3,1,2,0:T(8,128)S(1)} %fusion.70), channel_id=1, source_target_pairs={{0,4},{4,8},{8,12},{12,16},{16,20},{20,24},{24,28},{1,5},{5,9},{9,... | collective-permute-start | bytes 49160 | tf_op jit(solution)/shard_map/ppermute | solution.py:18
  50.1 1.6 collective-permute-done.7
  53.1 5.8 %collective-permute-start.9 = (f32[1,4,1,32,32]{4,3,1,2,0:T(8,128)S(1)}, f32[1,4,1,32,32]{4,3,1,2,0:T(8,128)S(1)}, u32[]{:S(2)}, u32[]{:S(2)}) collective-permute-start(f32[1,4,1,32,32]{4,3,1,2,0:T(8,128)S(1)} %fusion.81), channel_id=1, source_target_pairs={{0,4},{4,8},{8,12},{12,16},{16,20},{20,24},{24,28},{1,5},{5,9},{9,... | collective-permute-start | bytes 49160 | tf_op jit(solution)/shard_map/ppermute | solution.py:18
  59.2 1.6 collective-permute-done.9
  62.2 5.8 %collective-permute-start.11 = (f32[1,4,1,32,32]{4,3,1,2,0:T(8,128)S(1)}, f32[1,4,1,32,32]{4,3,1,2,0:T(8,128)S(1)}, u32[]{:S(2)}, u32[]{:S(2)}) collective-permute-start(f32[1,4,1,32,32]{4,3,1,2,0:T(8,128)S(1)} %fusion.92), channel_id=1, source_target_pairs={{0,4},{4,8},{8,12},{12,16},{16,20},{20,24},{24,28},{1,5},{5,9},{9,... | collective-permute-start | bytes 49160 | tf_op jit(solution)/shard_map/ppermute | solution.py:18
  68.3 1.6 collective-permute-done.11
  71.3 5.8 %collective-permute-start.13 = (f32[1,4,1,32,32]{4,3,1,2,0:T(8,128)S(1)}, f32[1,4,1,32,32]{4,3,1,2,0:T(8,128)S(1)}, u32[]{:S(2)}, u32[]{:S(2)}) collective-permute-start(f32[1,4,1,32,32]{4,3,1,2,0:T(8,128)S(1)} %fusion.103), channel_id=1, source_target_pairs={{0,4},{4,8},{8,12},{12,16},{16,20},{20,24},{24,28},{1,5},{5,9},{9,... | collective-permute-start | bytes 49160 | tf_op jit(solution)/shard_map/ppermute | solution.py:18
  77.4 1.6 collective-permute-done.13
  80.7 5.8 %collective-permute-start.15 = (f32[1,4,1,64,64]{4,3,2,1,0:T(8,128)S(1)}, f32[1,4,1,64,64]{4,3,2,1,0:T(8,128)S(1)}, u32[]{:S(2)}, u32[]{:S(2)}) collective-permute-start(f32[1,4,1,64,64]{4,3,2,1,0:T(8,128)S(1)} %get-tuple-element.12), channel_id=1, source_target_pairs={{0,4},{4,8},{8,12},{12,16},{16,20},{20,24},{24,28},{1,5},{5,9},{9,... | collective-permute-start | bytes 196616 | tf_op jit(solution)/shard_map/ppermute | solution.py:18
  87.5 2.3 %collective-permute-done.15 = f32[1,4,1,64,64]{4,3,2,1,0:T(8,128)S(1)} collective-permute-done((f32[1,4,1,64,64]{4,3,2,1,0:T(8,128)S(1)}, f32[1,4,1,64,64]{4,3,2,1,0:T(8,128)S(1)}, u32[]{:S(2)}, u32[]{:S(2)}) %collective-permute-start.15) | collective-permute-done | bytes 65568 | tf_op jit(solution)/shard_map/ppermute | solution.py:18
  90.9 1.3 collective-permute-start.16
  92.2 5.1 %collective-permute-start.17 = (f32[1,4,1,128,128]{4,3,2,1,0:T(8,128)S(1)}, f32[1,4,1,128,128]{4,3,2,1,0:T(8,128)S(1)}, u32[]{:S(2)}, u32[]{:S(2)}) collective-permute-start(f32[1,4,1,128,128]{4,3,2,1,0:T(8,128)S(1)} %get-tuple-element.8), channel_id=1, source_target_pairs={{0,4},{4,8},{8,12},{12,16},{16,20},{20,24},{24,28},{1,5},{5,9},{9,... | collective-permute-start | bytes 786440 | tf_op jit(solution)/shard_map/ppermute | solution.py:18
  97.3 2.4 %collective-permute-done.16 = f32[1,4,1,128,128]{4,3,2,1,0:T(8,128)S(1)} collective-permute-done((f32[1,4,1,128,128]{4,3,2,1,0:T(8,128)S(1)}, f32[1,4,1,128,128]{4,3,2,1,0:T(8,128)S(1)}, u32[]{:S(2)}, u32[]{:S(2)}) %collective-permute-start.16) | collective-permute-done | bytes 262176 | tf_op jit(solution)/shard_map/ppermute | solution.py:21
  99.7 4.3 %collective-permute-done.17 = f32[1,4,1,128,128]{4,3,2,1,0:T(8,128)S(1)} collective-permute-done((f32[1,4,1,128,128]{4,3,2,1,0:T(8,128)S(1)}, f32[1,4,1,128,128]{4,3,2,1,0:T(8,128)S(1)}, u32[]{:S(2)}, u32[]{:S(2)}) %collective-permute-start.17) | collective-permute-done | bytes 262176 | tf_op jit(solution)/shard_map/ppermute | solution.py:18
  104.0 1.8 %fusion.175 = (bf16[1,4,4,128,128]{4,3,2,1,0:T(8,128)(2,1)S(1)}, f32[1,4,4,128,128]{4,3,2,1,0:T(8,128)}) fusion(f32[1,4,4,128,128]{4,3,2,1,0:T(8,128)S(1)} %fusion.181, f32[4,128,128]{2,1,0:T(8,128)S(1)} %multiply_add_fusion, f32[1,4,4,128,128]{4,3,2,1,0:T(8,128)S(1)} %copy-done, f32[1,4,1,128,128]{4,3,2,1,0:T(8,128)S(1)} %collective-permute-done.17, ...), kind=kLoop, calls=%fused_computation.234 | loop fusion | flops 4456448 | bytes 4718592 | tf_op jit(solution)/shard_map/convert_element_type | solution.py:104
  105.8 6.7 %collective-permute-done.18 = bf16[1,4,4,128,128]{4,3,2,1,0:T(8,128)(2,1)S(1)} collective-permute-done((bf16[1,4,4,128,128]{4,3,2,1,0:T(8,128)(2,1)S(1)}, bf16[1,4,4,128,128]{4,3,2,1,0:T(8,128)(2,1)S(1)}, u32[]{:S(2)}, u32[]{:S(2)}) %collective-permute-start.18) | collective-permute-done | bytes 524320 | tf_op jit(solution)/shard_map/ppermute | solution.py:29
  112.5 1.9 %collective-permute-start.19 = (bf16[1,4,4,128,128]{4,3,2,1,0:T(8,128)(2,1)S(1)}, bf16[1,4,4,128,128]{4,3,2,1,0:T(8,128)(2,1)S(1)}, u32[]{:S(2)}, u32[]{:S(2)}) collective-permute-start(bf16[1,4,4,128,128]{4,3,2,1,0:T(8,128)(2,1)S(1)} %collective-permute-done.18), channel_id=1, source_target_pairs={{0,3},{1,0},{2,1},{3,2},{4,7},{5,4},{6,5},{7,6},{8,11},{9,8},{10,9... | collective-permute-start | bytes 1572872 | tf_op jit(solution)/shard_map/ppermute | solution.py:29
  114.4 6.7 %collective-permute-done.19 = bf16[1,4,4,128,128]{4,3,2,1,0:T(8,128)(2,1)S(1)} collective-permute-done((bf16[1,4,4,128,128]{4,3,2,1,0:T(8,128)(2,1)S(1)}, bf16[1,4,4,128,128]{4,3,2,1,0:T(8,128)(2,1)S(1)}, u32[]{:S(2)}, u32[]{:S(2)}) %collective-permute-start.19) | collective-permute-done | bytes 524320 | tf_op jit(solution)/shard_map/ppermute | solution.py:29
  125.4 48.2 %psum.7 = f32[4,4]{1,0:T(4,128)S(1)} all-reduce(f32[4,4]{1,0:T(4,128)S(1)} %dynamic_update_slice.19), channel_id=1, replica_groups=mesh['brick'=8,'vec'=4] {'brick','vec'}, use_global_device_ids=true, to_apply=%region_0.1 | all-reduce | flops 16 | bytes 128 | tf_op jit(solution)/shard_map/psum | solution.py:127
  (60 shorter events, 18.0 us)
Async XLA Ops:
  1.6 9.2 %copy-start.1 = (f32[4,128,128]{2,1,0:T(8,128)S(1)}, f32[4,128,128]{2,1,0:T(8,128)}, u32[]{:S(2)}) copy-start(f32[4,128,128]{2,1,0:T(8,128)} %param.3) | copy-start | bytes 786436
  3.0 17.2 %copy-start = (f32[1,4,4,128,128]{4,3,2,1,0:T(8,128)S(1)}, f32[1,4,4,128,128]{4,3,2,1,0:T(8,128)}, u32[]{:S(2)}) copy-start(f32[1,4,4,128,128]{4,3,2,1,0:T(8,128)} %param.2) | copy-start | bytes 3145732
  3.1 11.4 %collective-permute-start = (f32[1,4,1,128,128]{4,3,2,1,0:T(8,128)S(1)}, f32[1,4,1,128,128]{4,3,2,1,0:T(8,128)}, u32[]{:S(2)}, u32[]{:S(2)}) collective-permute-start(f32[1,4,1,128,128]{4,3,2,1,0:T(8,128)S(1)} %get-tuple-element.9), channel_id=1, source_target_pairs={{4,0},{8,4},{12,8},{16,12},{20,16},{24,20},{28,24},{5,1},{9,5},{13... | collective-permute-start | bytes 786440 | tf_op jit(solution)/shard_map/ppermute | solution.py:21
  4.5 15.7 %collective-permute-start.1 = (f32[1,4,1,128,128]{4,3,2,1,0:T(8,128)S(1)}, f32[1,4,1,128,128]{4,3,2,1,0:T(8,128)}, u32[]{:S(2)}, u32[]{:S(2)}) collective-permute-start(f32[1,4,1,128,128]{4,3,2,1,0:T(8,128)S(1)} %get-tuple-element.10), channel_id=1, source_target_pairs={{0,4},{4,8},{8,12},{12,16},{16,20},{20,24},{24,28},{1,5},{5,9},{9,... | collective-permute-start | bytes 786440 | tf_op jit(solution)/shard_map/ppermute | solution.py:18
  22.8 8.2 %collective-permute-start.2 = (f32[1,4,1,64,64]{4,3,2,1,0:T(8,128)S(1)}, f32[1,4,1,64,64]{4,3,2,1,0:T(8,128)S(1)}, u32[]{:S(2)}, u32[]{:S(2)}) collective-permute-start(f32[1,4,1,64,64]{4,3,2,1,0:T(8,128)S(1)} %get-tuple-element.13), channel_id=1, source_target_pairs={{4,0},{8,4},{12,8},{16,12},{20,16},{24,20},{28,24},{5,1},{9,5},{13... | collective-permute-start | bytes 196616 | tf_op jit(solution)/shard_map/ppermute | solution.py:21
  24.1 9.8 %collective-permute-start.3 = (f32[1,4,1,64,64]{4,3,2,1,0:T(8,128)S(1)}, f32[1,4,1,64,64]{4,3,2,1,0:T(8,128)S(1)}, u32[]{:S(2)}, u32[]{:S(2)}) collective-permute-start(f32[1,4,1,64,64]{4,3,2,1,0:T(8,128)S(1)} %get-tuple-element.14), channel_id=1, source_target_pairs={{0,4},{4,8},{8,12},{12,16},{16,20},{20,24},{24,28},{1,5},{5,9},{9,... | collective-permute-start | bytes 196616 | tf_op jit(solution)/shard_map/ppermute | solution.py:18
  34.7 6.7 %collective-permute-start.4 = (f32[1,4,1,32,32]{4,3,1,2,0:T(8,128)S(1)}, f32[1,4,1,32,32]{4,3,1,2,0:T(8,128)S(1)}, u32[]{:S(2)}, u32[]{:S(2)}) collective-permute-start(f32[1,4,1,32,32]{4,3,1,2,0:T(8,128)S(1)} %fusion.130), channel_id=1, source_target_pairs={{4,0},{8,4},{12,8},{16,12},{20,16},{24,20},{28,24},{5,1},{9,5},{13... | collective-permute-start | bytes 49160 | tf_op jit(solution)/shard_map/ppermute | solution.py:21
  36.0 7.2 %collective-permute-start.5 = (f32[1,4,1,32,32]{4,3,1,2,0:T(8,128)S(1)}, f32[1,4,1,32,32]{4,3,1,2,0:T(8,128)S(1)}, u32[]{:S(2)}, u32[]{:S(2)}) collective-permute-start(f32[1,4,1,32,32]{4,3,1,2,0:T(8,128)S(1)} %fusion.130), channel_id=1, source_target_pairs={{0,4},{4,8},{8,12},{12,16},{16,20},{20,24},{24,28},{1,5},{5,9},{9,... | collective-permute-start | bytes 49160 | tf_op jit(solution)/shard_map/ppermute | solution.py:18
  43.2 6.8 %collective-permute-start.6 = (f32[1,4,1,32,32]{4,3,1,2,0:T(8,128)S(1)}, f32[1,4,1,32,32]{4,3,1,2,0:T(8,128)S(1)}, u32[]{:S(2)}, u32[]{:S(2)}) collective-permute-start(f32[1,4,1,32,32]{4,3,1,2,0:T(8,128)S(1)} %fusion.70), channel_id=1, source_target_pairs={{4,0},{8,4},{12,8},{16,12},{20,16},{24,20},{28,24},{5,1},{9,5},{13... | collective-permute-start | bytes 49160 | tf_op jit(solution)/shard_map/ppermute | solution.py:21
  44.5 7.1 %collective-permute-start.7 = (f32[1,4,1,32,32]{4,3,1,2,0:T(8,128)S(1)}, f32[1,4,1,32,32]{4,3,1,2,0:T(8,128)S(1)}, u32[]{:S(2)}, u32[]{:S(2)}) collective-permute-start(f32[1,4,1,32,32]{4,3,1,2,0:T(8,128)S(1)} %fusion.70), channel_id=1, source_target_pairs={{0,4},{4,8},{8,12},{12,16},{16,20},{20,24},{24,28},{1,5},{5,9},{9,... | collective-permute-start | bytes 49160 | tf_op jit(solution)/shard_map/ppermute | solution.py:18
  51.8 7.4 %collective-permute-start.8 = (f32[1,4,1,32,32]{4,3,1,2,0:T(8,128)S(1)}, f32[1,4,1,32,32]{4,3,1,2,0:T(8,128)S(1)}, u32[]{:S(2)}, u32[]{:S(2)}) collective-permute-start(f32[1,4,1,32,32]{4,3,1,2,0:T(8,128)S(1)} %fusion.81), channel_id=1, source_target_pairs={{4,0},{8,4},{12,8},{16,12},{20,16},{24,20},{28,24},{5,1},{9,5},{13... | collective-permute-start | bytes 49160 | tf_op jit(solution)/shard_map/ppermute | solution.py:21
  53.1 7.7 %collective-permute-start.9 = (f32[1,4,1,32,32]{4,3,1,2,0:T(8,128)S(1)}, f32[1,4,1,32,32]{4,3,1,2,0:T(8,128)S(1)}, u32[]{:S(2)}, u32[]{:S(2)}) collective-permute-start(f32[1,4,1,32,32]{4,3,1,2,0:T(8,128)S(1)} %fusion.81), channel_id=1, source_target_pairs={{0,4},{4,8},{8,12},{12,16},{16,20},{20,24},{24,28},{1,5},{5,9},{9,... | collective-permute-start | bytes 49160 | tf_op jit(solution)/shard_map/ppermute | solution.py:18
  60.9 7.4 %collective-permute-start.10 = (f32[1,4,1,32,32]{4,3,1,2,0:T(8,128)S(1)}, f32[1,4,1,32,32]{4,3,1,2,0:T(8,128)S(1)}, u32[]{:S(2)}, u32[]{:S(2)}) collective-permute-start(f32[1,4,1,32,32]{4,3,1,2,0:T(8,128)S(1)} %fusion.92), channel_id=1, source_target_pairs={{4,0},{8,4},{12,8},{16,12},{20,16},{24,20},{28,24},{5,1},{9,5},{13... | collective-permute-start | bytes 49160 | tf_op jit(solution)/shard_map/ppermute | solution.py:21
  62.2 7.7 %collective-permute-start.11 = (f32[1,4,1,32,32]{4,3,1,2,0:T(8,128)S(1)}, f32[1,4,1,32,32]{4,3,1,2,0:T(8,128)S(1)}, u32[]{:S(2)}, u32[]{:S(2)}) collective-permute-start(f32[1,4,1,32,32]{4,3,1,2,0:T(8,128)S(1)} %fusion.92), channel_id=1, source_target_pairs={{0,4},{4,8},{8,12},{12,16},{16,20},{20,24},{24,28},{1,5},{5,9},{9,... | collective-permute-start | bytes 49160 | tf_op jit(solution)/shard_map/ppermute | solution.py:18
  70.0 7.4 %collective-permute-start.12 = (f32[1,4,1,32,32]{4,3,1,2,0:T(8,128)S(1)}, f32[1,4,1,32,32]{4,3,1,2,0:T(8,128)S(1)}, u32[]{:S(2)}, u32[]{:S(2)}) collective-permute-start(f32[1,4,1,32,32]{4,3,1,2,0:T(8,128)S(1)} %fusion.103), channel_id=1, source_target_pairs={{4,0},{8,4},{12,8},{16,12},{20,16},{24,20},{28,24},{5,1},{9,5},{13... | collective-permute-start | bytes 49160 | tf_op jit(solution)/shard_map/ppermute | solution.py:21
  71.3 7.7 %collective-permute-start.13 = (f32[1,4,1,32,32]{4,3,1,2,0:T(8,128)S(1)}, f32[1,4,1,32,32]{4,3,1,2,0:T(8,128)S(1)}, u32[]{:S(2)}, u32[]{:S(2)}) collective-permute-start(f32[1,4,1,32,32]{4,3,1,2,0:T(8,128)S(1)} %fusion.103), channel_id=1, source_target_pairs={{0,4},{4,8},{8,12},{12,16},{16,20},{20,24},{24,28},{1,5},{5,9},{9,... | collective-permute-start | bytes 49160 | tf_op jit(solution)/shard_map/ppermute | solution.py:18
  79.4 8.1 %collective-permute-start.14 = (f32[1,4,1,64,64]{4,3,2,1,0:T(8,128)S(1)}, f32[1,4,1,64,64]{4,3,2,1,0:T(8,128)S(1)}, u32[]{:S(2)}, u32[]{:S(2)}) collective-permute-start(f32[1,4,1,64,64]{4,3,2,1,0:T(8,128)S(1)} %get-tuple-element.11), channel_id=1, source_target_pairs={{4,0},{8,4},{12,8},{16,12},{20,16},{24,20},{28,24},{5,1},{9,5},{13... | collective-permute-start | bytes 196616 | tf_op jit(solution)/shard_map/ppermute | solution.py:21
  80.7 9.1 %collective-permute-start.15 = (f32[1,4,1,64,64]{4,3,2,1,0:T(8,128)S(1)}, f32[1,4,1,64,64]{4,3,2,1,0:T(8,128)S(1)}, u32[]{:S(2)}, u32[]{:S(2)}) collective-permute-start(f32[1,4,1,64,64]{4,3,2,1,0:T(8,128)S(1)} %get-tuple-element.12), channel_id=1, source_target_pairs={{0,4},{4,8},{8,12},{12,16},{16,20},{20,24},{24,28},{1,5},{5,9},{9,... | collective-permute-start | bytes 196616 | tf_op jit(solution)/shard_map/ppermute | solution.py:18
  90.9 8.8 %collective-permute-start.16 = (f32[1,4,1,128,128]{4,3,2,1,0:T(8,128)S(1)}, f32[1,4,1,128,128]{4,3,2,1,0:T(8,128)S(1)}, u32[]{:S(2)}, u32[]{:S(2)}) collective-permute-start(f32[1,4,1,128,128]{4,3,2,1,0:T(8,128)S(1)} %get-tuple-element.7), channel_id=1, source_target_pairs={{4,0},{8,4},{12,8},{16,12},{20,16},{24,20},{28,24},{5,1},{9,5},{13... | collective-permute-start | bytes 786440 | tf_op jit(solution)/shard_map/ppermute | solution.py:21
  92.2 11.8 %collective-permute-start.17 = (f32[1,4,1,128,128]{4,3,2,1,0:T(8,128)S(1)}, f32[1,4,1,128,128]{4,3,2,1,0:T(8,128)S(1)}, u32[]{:S(2)}, u32[]{:S(2)}) collective-permute-start(f32[1,4,1,128,128]{4,3,2,1,0:T(8,128)S(1)} %get-tuple-element.8), channel_id=1, source_target_pairs={{0,4},{4,8},{8,12},{12,16},{16,20},{20,24},{24,28},{1,5},{5,9},{9,... | collective-permute-start | bytes 786440 | tf_op jit(solution)/shard_map/ppermute | solution.py:18
  105.8 6.7 %collective-permute-start.18 = (bf16[1,4,4,128,128]{4,3,2,1,0:T(8,128)(2,1)S(1)}, bf16[1,4,4,128,128]{4,3,2,1,0:T(8,128)(2,1)S(1)}, u32[]{:S(2)}, u32[]{:S(2)}) collective-permute-start(bf16[1,4,4,128,128]{4,3,2,1,0:T(8,128)(2,1)S(1)} %get-tuple-element.5), channel_id=1, source_target_pairs={{0,3},{1,0},{2,1},{3,2},{4,7},{5,4},{6,5},{7,6},{8,11},{9,8},{10,9... | collective-permute-start | bytes 1572872 | tf_op jit(solution)/shard_map/ppermute | solution.py:29
  112.5 8.6 %collective-permute-start.19 = (bf16[1,4,4,128,128]{4,3,2,1,0:T(8,128)(2,1)S(1)}, bf16[1,4,4,128,128]{4,3,2,1,0:T(8,128)(2,1)S(1)}, u32[]{:S(2)}, u32[]{:S(2)}) collective-permute-start(bf16[1,4,4,128,128]{4,3,2,1,0:T(8,128)(2,1)S(1)} %collective-permute-done.18), channel_id=1, source_target_pairs={{0,3},{1,0},{2,1},{3,2},{4,7},{5,4},{6,5},{7,6},{8,11},{9,8},{10,9... | collective-permute-start | bytes 1572872 | tf_op jit(solution)/shard_map/ppermute | solution.py:29
where the time goes:
time: 175 us; the launch traced here: 174 us
  starting transfers between devices  63.6 us (36%)
  blocking collectives  48.2 us (28%)
  waiting for transfers between devices  46.6 us (27%)
  other arithmetic  8.18 us (5%)
  local copies, waits for them, and re-layouts  4.08 us (2%)
  matrix products  1.75 us (1%)
    ppermute x9, starting transfers between devices, extended(): lax.ppermute(lax.slice_in_dim(block, block.shape[dim] - width, None, axis...  49.9 us
    psum x1, blocking collectives, local(): total = lax.psum(contributions, ('brick', 'vec'))  48.2 us
    ppermute x9, waiting for transfers between devices, extended(): lax.ppermute(lax.slice_in_dim(block, block.shape[dim] - width, None, axis...  23.3 us
    ppermute x2, waiting for transfers between devices, passed_along(): return lax.ppermute(value, axis, pairs)  13.4 us
    ppermute x9, starting transfers between devices, extended(): lax.ppermute(lax.slice_in_dim(block, 0, width, axis=dim), axis, backward)  11.8 us
    ppermute x9, waiting for transfers between devices, extended(): lax.ppermute(lax.slice_in_dim(block, 0, width, axis=dim), axis, backward)  9.93 us
  transfers between devices with their start and end apart: 20, of which 20 were waited for; matrix products, arithmetic and copies ran while one was open for 0% of the time, Pallas kernels for 0%

commit v1 on v0

v1 whole, which is shorter than its diff:
```python
import functools

import jax
import jax.numpy as jnp
from jax import lax
from jax.experimental import pallas as pl
from jax.experimental.pallas import tpu as pltpu
from jax.sharding import PartitionSpec as P

SWEEPS = 6
shift_value = 0.1
damping = 0.8
keep = 1.0 - damping
F32 = jnp.float32
BF16 = jnp.bfloat16
MESH = pl.DeviceIdType.MESH


def rolled_sides(x, axis, width):
    size = x.shape[axis]
    place = lax.broadcasted_iota(jnp.int32, x.shape, axis) % width
    low = jnp.where(place == 0, 0.0, pltpu.roll(x, 1, axis))
    high = jnp.where(place == width - 1, 0.0, pltpu.roll(x, size - 1, axis))
    return low + high


def in_plane(x, width):
    return rolled_sides(x, 0, x.shape[0]) + rolled_sides(x, 1, width)


def split_dot(x, table):
    head = x.astype(BF16)
    tail = (x - head.astype(F32)).astype(BF16)
    return jnp.dot(head, table, preferred_element_type=F32) + jnp.dot(
        tail, table, preferred_element_type=F32
    )


def merge_table(parts, lanes):
    row = lax.broadcasted_iota(jnp.int32, (parts * lanes, lanes), 0)
    col = lax.broadcasted_iota(jnp.int32, (parts * lanes, lanes), 1)
    return jnp.where(row // 2 == col, 1.0, 0.0).astype(BF16)


def spread_table(parts, lanes):
    row = lax.broadcasted_iota(jnp.int32, (lanes, parts * lanes), 0)
    col = lax.broadcasted_iota(jnp.int32, (lanes, parts * lanes), 1)
    return jnp.where(col // 2 == row, 1.0, 0.0).astype(BF16)


def repeat_table(lanes, source, width):
    row = lax.broadcasted_iota(jnp.int32, (lanes, lanes), 0)
    col = lax.broadcasted_iota(jnp.int32, (lanes, lanes), 1)
    hit = (row // 2 == col % width) & (row < source)
    return jnp.where(hit, 1.0, 0.0).astype(BF16)


def kernel(bricks, group, reach, rhs, kap, out, gram, xp, g0, x0s, x0h, tmp, ktmp, x1p, x1s,
           x1h, b1s, k1s, q1s, q1h, t1, x2s, x2h, q2s, q2h, t2, w1, w0, zb, zr, part, g1h, rows_s,
           g2h, sems_r, sems_s):
    fields, planes, ys, zs = rhs.shape[1:]
    pairs = fields // 2
    y1, y2 = ys // 2, ys // 4
    width1, width2 = zs // 2, zs // 4
    half = planes // 2
    b = lax.axis_index("brick")
    v = lax.axis_index("vec")
    has = (b > 0, b < bricks - 1)
    side = (-1, 1)
    counter = [0]
    sends = []

    def copy(src, dst, sem, brick, vec):
        return pltpu.make_async_remote_copy(
            src_ref=src, dst_ref=dst, send_sem=sems_s.at[sem], recv_sem=sems_r.at[sem],
            device_id=(brick, vec), device_id_type=MESH)

    def begin(cond, src, dst, sem, brick, vec):
        made = copy(src, dst, sem, brick, vec)
        if cond is None:
            made.start()
        else:
            pl.when(cond)(made.start)
        sends.append((cond, made))

    def arrive(cond, dst, sem):
        waiter = copy(dst, dst, sem, b, v)
        if cond is None:
            waiter.wait_recv()
        else:
            pl.when(cond)(waiter.wait_recv)

    def number(count):
        base = counter[0]
        counter[0] += count
        return base

    sem_x0 = number(2 * fields)
    sem_x1 = number(4)
    sem_q1 = number(2)
    sem_x2 = number(2 * reach + 1)
    sem_q2 = number(2 * reach + 1)
    sem_z = number(group)
    sem_g1 = number(group)
    sem_g2 = number(bricks)

    barrier = pltpu.get_barrier_semaphore()
    for step in range(1, bricks):
        pl.semaphore_signal(barrier, inc=1, device_id=((b + step) % bricks, v),
                            device_id_type=MESH)
    for step in range(1, group):
        pl.semaphore_signal(barrier, inc=1, device_id=(b, (v + step) % group),
                            device_id_type=MESH)

    for p in range(planes):
        g0[p] = damping / (shift_value + 6.0 * kap[p])
    for f in range(fields):
        for p in range(planes):
            x = g0[p] * rhs[0, f, p]
            xp[f, p + 1] = x
            if p == 0:
                x0s[0, f] = x.astype(BF16)
            if p == planes - 1:
                x0s[1, f] = x.astype(BF16)
    for s in range(2):
        @pl.when(jnp.logical_not(has[s]))
        def _(s=s):
            x0h[s] = jnp.zeros_like(x0h.at[s])
            x1h[s] = jnp.zeros_like(x1h.at[s])
            q1h[s] = jnp.zeros_like(q1h.at[s])
    for off in range(-reach, reach + 1):
        if off:
            @pl.when((b + off < 0) | (b + off >= bricks))
            def _(off=off):
                x2h[off + reach] = jnp.zeros_like(x2h.at[off + reach])
                q2h[off + reach] = jnp.zeros_like(q2h.at[off + reach])

    pl.semaphore_wait(barrier, bricks - 1 + group - 1)
    for f in range(fields):
        for s in range(2):
            begin(has[s], x0s.at[s, f], x0h.at[1 - s, f], sem_x0 + (1 - s) * fields + f,
                  b + side[s], v)

    merge = merge_table(2, zs)
    spread = spread_table(2, zs)
    for h in range(half):
        ktmp[h] = kap[2 * h] + kap[2 * h + 1]
    k1 = []
    for h in range(half):
        summed = ktmp.at[h][pl.ds(0, y1, stride=2), :] + ktmp.at[h][pl.ds(1, y1, stride=2), :]
        k = split_dot(summed, repeat_table(zs, zs, width1)) * 0.125
        k1s[h] = k
        k1.append(k)
    gd1 = [damping / (shift_value + 6.0 * 0.25 * k) for k in k1]
    for h in range(half):
        q1s[h] = gd1[h] * (0.25 * k1[h])
    t1[0] = k1[0] + k1[1]
    summed = t1.at[0][pl.ds(0, y2, stride=2), :] + t1.at[0][pl.ds(1, y2, stride=2), :]
    k2 = split_dot(summed, repeat_table(zs, width1, width2)) * 0.125
    gd2 = damping / (shift_value + 6.0 * 0.0625 * k2)
    q2s[...] = gd2 * (0.0625 * k2)
    for s in range(2):
        begin(has[s], q1s.at[0 if s == 0 else half - 1], q1h.at[1 - s], sem_q1 + 1 - s,
              b + side[s], v)
    for size in range(1, reach + 1):
        for off in (-size, size):
            begin((b + off >= 0) & (b + off < bricks), q2s, q2h.at[reach - off],
                  sem_q2 + reach - off, b + off, v)

    for pair in range(pairs):
        halved = [[None] * 2 for _ in range(half)]
        for inner in range(2):
            f = 2 * pair + inner
            for s in range(2):
                arrive(has[s], x0h.at[s, f], sem_x0 + s * fields + f)
            xp[f, 0] = x0h[0, f].astype(F32)
            xp[f, planes + 1] = x0h[1, f].astype(F32)
            for h in range(half):
                total = None
                for p in (2 * h, 2 * h + 1):
                    around = in_plane(xp[f, p + 1], zs) + xp[f, p] + xp[f, p + 2]
                    resid = keep * rhs[0, f, p] + kap[p] * around
                    total = resid if total is None else total + resid
                tmp[f, h] = total
                view = tmp.at[f, h]
                halved[h][inner] = view[pl.ds(0, y1, stride=2), :] + view[pl.ds(1, y1, stride=2), :]
        for h in range(half):
            b1 = split_dot(jnp.concatenate(halved[h], axis=1), merge) * 0.125
            b1s[pair, h] = b1
            x1 = gd1[h] * b1
            x1p[pair, h + 2] = x1
            x1s[h, pair] = x1.astype(x1s.dtype)

    for order in range(half):
        for s in range(2):
            plane = order if s == 0 else half - 1 - order
            begin(has[s], x1s.at[plane], x1h.at[1 - s, order], sem_x1 + (1 - s) * 2 + order,
                  b + side[s], v)
    for s in range(2):
        arrive(has[s], x1h.at[s, 0], sem_x1 + s * 2)
    halved = []
    for pair in range(pairs):
        x1p[pair, 1] = x1h[0, 0, pair].astype(F32)
        x1p[pair, half + 2] = x1h[1, 0, pair].astype(F32)
        total = None
        for h in range(half):
            around = in_plane(x1p[pair, h + 2], width1) + x1p[pair, h + 1] + x1p[pair, h + 3]
            resid = keep * b1s[pair, h] + 0.25 * k1s[h] * around
            total = resid if total is None else total + resid
        t1[pair] = total
        view = t1.at[pair]
        halved.append(view[pl.ds(0, y2, stride=2), :] + view[pl.ds(1, y2, stride=2), :])
    b2 = split_dot(jnp.concatenate(halved, axis=1), merge) * 0.125
    x20 = gd2 * b2
    x2s[...] = x20.astype(x2s.dtype)
    for size in range(reach, 0, -1):
        for off in (-size, size):
            begin((b + off >= 0) & (b + off < bricks), x2s, x2h.at[reach - off],
                  sem_x2 + reach - off, b + off, v)
    for s in range(2):
        arrive(has[s], x1h.at[s, 1], sem_x1 + s * 2 + 1)
        arrive(has[s], q1h.at[s], sem_q1 + s)
        for pair in range(pairs):
            x1p[pair, 0 if s == 0 else half + 3] = x1h[s, 1, pair].astype(F32)
    for off in range(-reach, reach + 1):
        if off:
            cond = (b + off >= 0) & (b + off < bricks)
            arrive(cond, q2h.at[off + reach], sem_q2 + off + reach)
            arrive(cond, x2h.at[off + reach], sem_x2 + off + reach)

    start = {off: x2h[off + reach].astype(F32) for off in range(-reach, reach + 1) if off}
    start[0] = x20
    level2 = dict(start)
    zero = jnp.zeros_like(x20)
    for sweep in range(1, SWEEPS):
        wide = SWEEPS - sweep
        after = {}
        for off in range(-min(wide, reach), min(wide, reach) + 1):
            x = level2[off]
            around = in_plane(x, width2) + level2.get(off - 1, zero) + level2.get(off + 1, zero)
            coeff = q2s[...] if off == 0 else q2h[off + reach]
            after[off] = keep * x + start[off] + coeff * around
        level2 = after

    own1 = [[x1p[pair, i] for i in range(half + 4)] for pair in range(pairs)]
    fixed = [[None] * (half + 4) for _ in range(pairs)]
    for off in (-1, 0, 1):
        wide = split_dot(level2[off], spread)
        for pair in range(pairs):
            view = t2.at[off + 1, pair]
            piece = wide[:, pair * zs:(pair + 1) * zs]
            view[pl.ds(0, y2, stride=2), :] = piece
            view[pl.ds(1, y2, stride=2), :] = piece
            for h in range(half):
                i = (off + 1) * half + h
                fixed[pair][i] = own1[pair][i] + view[...]
    for i in range(1, half + 3):
        coeff = q1h[0] if i == 1 else q1h[1] if i == half + 2 else q1s[i - 2]
        for pair in range(pairs):
            around = in_plane(fixed[pair][i], width1) + fixed[pair][i - 1] + fixed[pair][i + 1]
            smooth = keep * fixed[pair][i] + own1[pair][i] + coeff * around
            wide = split_dot(smooth, spread)
            w1[2 * pair, i - 1] = wide[:, :zs]
            w1[2 * pair + 1, i - 1] = wide[:, zs:]

    units = fields * planes
    share = units // group

    def correct(f):
        for i in range(half + 2):
            view = w0.at[i]
            piece = w1[f, i]
            view[pl.ds(0, y1, stride=2), :] = piece
            view[pl.ds(1, y1, stride=2), :] = piece
            wide = view[...]
            for slot in (2 * i - 1, 2 * i):
                if 0 <= slot <= planes + 1:
                    xp[f, slot] = xp[f, slot] + wide

    whole_fields = share % planes == 0
    if not whole_fields:
        for f in range(fields):
            correct(f)
    moves = [(dx, dc) for dx in range(group // 2 - 1, -1, -1) for dc in range(2)]
    moves = [m for m in moves if m != (0, 0)] + [(0, 0)]
    for index, (dx, dc) in enumerate(moves):
        owner = (v // 2 + dx) % (group // 2) * 2 + (v % 2 + dc) % 2
        if whole_fields:
            for i in range(share // planes):
                correct(owner * (share // planes) + i)
        for i in range(share):
            unit = owner * share + i
            f, p = unit // planes, unit % planes
            if whole_fields:
                f, p = owner * (share // planes) + i // planes, i % planes
            x = xp[f, p + 1]
            around = in_plane(x, zs) + xp[f, p] + xp[f, p + 2]
            result = keep * x + g0[p] * (rhs[0, f, p] + kap[p] * around)
            out[0, f, p] = result
            if (dx, dc) == (0, 0):
                zr[v, i] = result.astype(BF16)
            else:
                zb[index, i] = result.astype(BF16)
        if (dx, dc) != (0, 0):
            begin(None, zb.at[index], zr.at[v], sem_z + index, b, owner)
    for index, (dx, dc) in enumerate(moves):
        if (dx, dc) != (0, 0):
            source = (v // 2 + group // 2 - dx) % (group // 2) * 2 + (v % 2 + dc) % 2
            arrive(None, zr.at[source], sem_z + index)

    rows = 16
    keys = [(i, j) for i in range(group) for j in range(i, group)]
    per = ys // rows

    def products(step, totals):
        unit = step // per
        first = pl.multiple_of(step % per * rows, rows)
        values = [zr[i, unit, pl.ds(first, rows), :].astype(F32) for i in range(group)]
        return tuple(
            total + (values[i] * values[j]).reshape(rows // 8, 8, zs).sum(axis=0)
            for total, (i, j) in zip(totals, keys))

    totals = lax.fori_loop(0, share * per, products,
                           tuple(jnp.zeros((8, zs), F32) for _ in keys), unroll=4)
    part[...] = jnp.zeros_like(part)
    for (i, j), total in zip(keys, totals):
        line = jnp.sum(total, axis=0, keepdims=True)
        part[i, pl.ds(j, 1), :] = line
        if i != j:
            part[j, pl.ds(i, 1), :] = line
    for step in range(1, group):
        peer = (v + step) % group
        begin(None, part.at[peer], g1h.at[step], sem_g1 + step, b, peer)
    mine = part[v]
    for step in range(1, group):
        arrive(None, g1h.at[step], sem_g1 + step)
        mine = mine + g1h[step]
    rows_s[...] = mine
    for step in range(1, bricks):
        begin(None, rows_s, g2h.at[step], sem_g2 + step, (b + step) % bricks, v)
    for step in range(1, bricks):
        arrive(None, g2h.at[step], sem_g2 + step)
        mine = mine + g2h[step]
    sums = jnp.sum(mine, axis=1, keepdims=True)
    at_row = lax.broadcasted_iota(jnp.int32, mine.shape, 0)
    at_col = lax.broadcasted_iota(jnp.int32, mine.shape, 1)
    line = jnp.sum(jnp.where(at_row == at_col, sums, 0.0), axis=0, keepdims=True)
    gram[...] = line[:, :group]
    for cond, made in sends:
        if cond is None:
            made.wait_send()
        else:
            pl.when(cond)(made.wait_send)


def local(bricks, group, right_side, diffusivity):
    fields, planes, ys, zs = right_side.shape[1:]
    assert right_side.shape[0] == 1 and planes == 4 and zs == 128 and fields == 4
    pairs, half = fields // 2, planes // 2
    y1, y2 = ys // 2, ys // 4
    reach = min(SWEEPS, bricks - 1)
    units = fields * planes
    share = units // group
    tall = max(8, group)
    slots = 2 * reach + 1
    count = 2 * fields + 6 + 2 * slots + 2 * group + bricks
    vm = pltpu.VMEM
    return pl.pallas_call(
        functools.partial(kernel, bricks, group, reach),
        out_shape=(
            jax.ShapeDtypeStruct(right_side.shape, F32),
            jax.ShapeDtypeStruct((1, group), F32),
        ),
        in_specs=[pl.BlockSpec(memory_space=pltpu.VMEM)] * 2,
        out_specs=(pl.BlockSpec(memory_space=pltpu.VMEM),) * 2,
        scratch_shapes=[
            vm((fields, planes + 2, ys, zs), F32),
            vm((planes, ys, zs), F32),
            vm((2, fields, ys, zs), BF16),
            vm((2, fields, ys, zs), BF16),
            vm((fields, half, ys, zs), F32),
            vm((half, ys, zs), F32),
            vm((pairs, half + 4, y1, zs), F32),
            vm((half, pairs, y1, zs), F32),
            vm((2, half, pairs, y1, zs), F32),
            vm((pairs, half, y1, zs), F32),
            vm((half, y1, zs), F32),
            vm((half, y1, zs), F32),
            vm((2, y1, zs), F32),
            vm((pairs, y1, zs), F32),
            vm((y2, zs), F32),
            vm((slots, y2, zs), F32),
            vm((y2, zs), F32),
            vm((slots, y2, zs), F32),
            vm((3, pairs, y1, zs), F32),
            vm((fields, half + 2, y1, zs), F32),
            vm((half + 2, ys, zs), F32),
            vm((group, share, ys, zs), BF16),
            vm((group, share, ys, zs), BF16),
            vm((group, tall, zs), F32),
            vm((group, tall, zs), F32),
            vm((tall, zs), F32),
            vm((bricks, tall, zs), F32),
            pltpu.SemaphoreType.DMA((count,)),
            pltpu.SemaphoreType.DMA((count,)),
        ],
        compiler_params=pltpu.CompilerParams(
            collective_id=0, has_side_effects=True, vmem_limit_bytes=48 << 20
        ),
    )(right_side, diffusivity)


def solution(mesh):
    return jax.shard_map(
        functools.partial(local, mesh.shape["brick"], mesh.shape["vec"]),
        mesh=mesh,
        in_specs=(P("vec", None, "brick", None, None), P("brick", None, None)),
        out_specs=(P("vec", None, "brick", None, None), P("vec", None)),
        check_vma=False,
    )
```

time: 175 us -> 44.2 us (0.25)
  starting transfers between devices: 63.6 us -> 0 us
  blocking collectives: 48.2 us -> 0 us
  waiting for transfers between devices: 46.6 us -> 0 us
  Pallas kernels: 0 us -> 39.7 us
  other arithmetic: 8.18 us -> 0 us
  matrix products: 1.75 us -> 0 us
    ppermute x20 -> x0, starting transfers between devices: 63.6 us -> none  [the longest x9 49.9 us: extended(): lax.ppermute(lax.slice_in_dim(block, block.shape[dim] - width, None, axis...]
    psum x1 -> x0, blocking collectives: 48.2 us -> none  [local(): total = lax.psum(contributions, ('brick', 'vec'))]
    ppermute x20 -> x0, waiting for transfers between devices: 46.6 us -> none  [the longest x9 23.3 us: extended(): lax.ppermute(lax.slice_in_dim(block, block.shape[dim] - width, None, axis...]
    pallas_call x0 -> x1, Pallas kernels: none -> 39.7 us  [local(): pl.pallas_call(functools.partial(kernel, bricks, group, reach), out_shape...]
    unnamed x4 -> x6, local copies, waits for them, and re-layouts: 0.01 us -> 3.65 us
    dynamic_update_slice x5 -> x0, local copies, waits for them, and re-layouts: 2.43 us -> none  [the longest x2 0.92 us: local(): lax.dynamic_update_slice(contributions, pair_block, (row_start, col_start))]
    sub x2 -> x0, other arithmetic: 2.07 us -> none  [the longest x1 1.8 us: local(): resid0 = right_side - operate(slab_halo(level0), diffusivity, 1.0)]
    convert_element_type x1 -> x0, other arithmetic: 1.81 us -> none  [local(): rounded = precond.astype(jnp.bfloat16)]
  transfers between devices with their start and end apart: 20 -> 0, of which waited for: 20 -> 0; matrix products, arithmetic and copies ran while one was open for 0% -> 0% of each run, Pallas kernels for 0% -> 0%
where the time goes in v1:
time: 44.2 us; the launch traced here: 44 us
  Pallas kernels  39.7 us (90%)
  local copies, waits for them, and re-layouts  3.65 us (8%)
  between operations  0.65 us (1%)
    pallas_call x1, Pallas kernels, local(): pl.pallas_call(functools.partial(kernel, bricks, group, reach), out_shape...  39.7 us
    unnamed x6, local copies, waits for them, and re-layouts  3.65 us

profile of v1, /device:TPU:0, one launch (start us, length us, event | category | flops | bytes accessed | tf_op | source)
XLA Modules:
  0.0 44.0 jit_solution(12574336898676661956)
XLA Ops:
  0.6 0.0 copy-start
  0.6 1.2 %copy-done = f32[1,4,4,128,128]{4,3,2,1,0:T(8,128)S(1)} copy-done((f32[1,4,4,128,128]{4,3,2,1,0:T(8,128)S(1)}, f32[1,4,4,128,128]{4,3,2,1,0:T(8,128)}, u32[]{:S(2)}) %copy-start) | copy-done | bytes 1048600
  1.9 0.0 copy-start.1
  1.9 0.9 %copy-done.1 = f32[4,128,128]{2,1,0:T(8,128)S(1)} copy-done((f32[4,128,128]{2,1,0:T(8,128)S(1)}, f32[4,128,128]{2,1,0:T(8,128)}, u32[]{:S(2)}) %copy-start.1) | copy-done | bytes 262168
  2.8 39.7 %shard_map.41 = (f32[1,4,4,128,128]{4,3,2,1,0:T(8,128)S(1)}, f32[1,4]{1,0:T(1,128)S(1)}) custom-call(f32[1,4,4,128,128]{4,3,2,1,0:T(8,128)S(1)} %copy-done, f32[4,128,128]{2,1,0:T(8,128)S(1)} %copy-done.1), custom_call_target="tpu_custom_call" | custom-call | tf_op jit(solution)/shard_map/pallas_call | solution.py:368
  42.5 1.0 %copy.6 = f32[1,4,4,128,128]{4,3,2,1,0:T(8,128)} copy(f32[1,4,4,128,128]{4,3,2,1,0:T(8,128)S(1)} %get-tuple-element.4) | data formatting | bytes 2097152
  43.5 0.5 %copy.7 = f32[1,4]{1,0:T(1,128)} copy(f32[1,4]{1,0:T(1,128)S(1)} %get-tuple-element.5) | data formatting | bytes 32
Async XLA Ops:
  0.6 1.2 %copy-start = (f32[1,4,4,128,128]{4,3,2,1,0:T(8,128)S(1)}, f32[1,4,4,128,128]{4,3,2,1,0:T(8,128)}, u32[]{:S(2)}) copy-start(f32[1,4,4,128,128]{4,3,2,1,0:T(8,128)} %rhs.1) | copy-start | bytes 3145732
  1.9 0.9 %copy-start.1 = (f32[4,128,128]{2,1,0:T(8,128)S(1)}, f32[4,128,128]{2,1,0:T(8,128)}, u32[]{:S(2)}) copy-start(f32[4,128,128]{2,1,0:T(8,128)} %kap.1) | copy-start | bytes 786436
